TPU v7x, 512 devices: a whole 4x8x8 slice. The times are simulated.
512 devices in a mesh: blk: 32 (over y_hi, x, core), tp: 16 (over z, y_lo).
Axes of the slice: x: 4, y: 8 (y_hi: 4, y_lo: 2; y = y_hi * 2 + y_lo), z: 8, core: 2. Of those that a mesh axis runs over, the one named last changes fastest.
Arguments:
- tokens: bfloat16 [131072, 896], P(('blk', 'tp')), may hold values from -6 to 6
- cotangent: bfloat16 [131072, 896], P(('blk', 'tp')), may hold values from -0.59765625 to 0.59765625
- weights: bfloat16 [32, 2432, 3, 896], P('blk', 'tp'), may hold values from -6 to 6
- first_moment: bfloat16 [32, 2432, 3, 896], P('blk', 'tp'), may hold values from -0.1796875 to 0.1796875
- second_moment: bfloat16 [32, 2432, 3, 896], P('blk', 'tp'), may hold values from 0.0009994507 to 0.0099487305
Outputs:
- averaged: float32 [32, 2432, 3, 896], P('blk', 'tp')
All inputs are finite; a program needn't handle non-finite values.
Results may differ from a plain program's by a relative error of at most 0.0003.
Values may be sent and summed in bfloat16 or wider, within the bound.
A program may use at most 64 MiB of HBM per device.

v0:
```python
import jax
import jax.numpy as jnp
from jax import lax
from jax.sharding import PartitionSpec as P

STEP = 10


def shifted(block, axis, distance):
    devices = range(lax.axis_size(axis))
    route = [((i - distance) % len(devices), i) for i in devices]
    return lax.ppermute(block, axis, route)


def row_terms(xs, grads_out, rows, hidden_scale):
    width_scale = xs.shape[1] ** (-0.5)
    gate = (
        jnp.einsum("td,nd->tn", xs, rows[:, 0, :], preferred_element_type=jnp.float32) * width_scale
    )
    upper = (
        jnp.einsum("td,nd->tn", xs, rows[:, 1, :], preferred_element_type=jnp.float32) * width_scale
    )
    sigma = jax.nn.sigmoid(gate)
    swish = gate * sigma
    hidden = (swish * upper).astype(jnp.bfloat16)
    back = (
        jnp.einsum("td,nd->tn", grads_out, rows[:, 2, :], preferred_element_type=jnp.float32)
        * hidden_scale
    )
    dgate = (back * upper * sigma * (1.0 + gate * (1.0 - sigma))).astype(jnp.bfloat16)
    dupper = (back * swish).astype(jnp.bfloat16)
    grad_gate = jnp.einsum("tn,td->nd", dgate, xs, preferred_element_type=jnp.float32) * width_scale
    grad_upper = (
        jnp.einsum("tn,td->nd", dupper, xs, preferred_element_type=jnp.float32) * width_scale
    )
    grad_down = (
        jnp.einsum("tn,td->nd", hidden, grads_out, preferred_element_type=jnp.float32)
        * hidden_scale
    )
    return jnp.stack([grad_gate, grad_upper, grad_down], axis=1)


def on_device(tokens, cotangent, weights, first_moment, second_moment):
    own_rows = weights[0]
    local_units = own_rows.shape[0]
    hidden_scale = (local_units * lax.axis_size("tp")) ** (-0.5)
    all_tokens, all_cots = (
        lax.all_gather(tokens, "tp", axis=0, tiled=True),
        lax.all_gather(cotangent, "tp", axis=0, tiled=True),
    )
    grads = row_terms(all_tokens, all_cots, own_rows, hidden_scale)
    moment_one = 0.9 * first_moment[0].astype(jnp.float32) + 0.1 * grads
    moment_two = 0.95 * second_moment[0].astype(jnp.float32) + 0.05 * grads * grads
    correct_one = 1.0 - 0.9**STEP
    correct_two = 1.0 - 0.95**STEP
    master = own_rows.astype(jnp.float32)
    step_size = moment_one / correct_one / (jnp.sqrt(moment_two / correct_two) + 1e-08)
    updated = (master - 0.1 * (step_size + 0.1 * master))[None]
    previous = shifted(updated, "blk", 1)
    following = shifted(updated, "blk", -1)
    return (previous + updated + following) / 3.0


def solution(mesh):
    in_specs = (
        P(("blk", "tp"), None),
        P(("blk", "tp"), None),
        P("blk", "tp", None, None),
        P("blk", "tp", None, None),
        P("blk", "tp", None, None),
    )
    out_specs = P("blk", "tp", None, None)
    return jax.shard_map(
        on_device, mesh=mesh, in_specs=in_specs, out_specs=out_specs, check_vma=False
    )
```

profile of v0, /device:TPU:7, one launch (start us, length us, event | category | flops | bytes accessed | tf_op | source)
XLA Modules:
  0.0 412.8 jit_solution(5356604273082415112)
XLA Ops:
  6.5 0.0 all-gather.5.cloned.1.call-start
  6.5 0.7 all-gather.5.cloned.1.call-update
  7.3 0.0 all-gather.3.cloned.1.call-start
  7.3 0.7 all-gather.3.cloned.1.call-update
  8.0 172.2 %all-gather.5.cloned.1.call-done = bf16[4096,896]{1,0:T(8,128)(2,1)} async-done(((bf16[256,896]{1,0:T(8,128)(2,1)}), bf16[4096,896]{1,0:T(8,128)(2,1)}) %all-gather.5.cloned.1.call-update) | async-done | bytes 7340048 | tf_op jit(solution)/shard_map/all_gather | solution.py:48
  180.2 0.0 copy-start
  180.2 0.0 copy-start.3
  180.2 6.1 %convolution_multiply_fusion.1 = f32[4096,152]{0,1:T(8,128)S(1)} fusion(bf16[4096,896]{1,0:T(8,128)(2,1)} %all-gather.5.cloned.1.call-done, bf16[152,3,896]{2,0,1:T(8,128)(2,1)} %bitcast.24), kind=kOutput, calls=%fused_computation.1 | convolution fusion | flops 1116307456 | bytes 10102784 | tf_op jit(solution)/shard_map/td,nd->tn/dot_general | solution.py:21
  186.3 0.0 copy-done
  186.3 0.0 copy-done.3
  186.3 4.3 %convolution_multiply_fusion = f32[4096,152]{0,1:T(8,128)} fusion(bf16[4096,896]{1,0:T(8,128)(2,1)S(1)} %copy-done, bf16[152,3,896]{2,0,1:T(8,128)(2,1)S(1)} %bitcast.25), kind=kOutput, calls=%fused_computation | convolution fusion | flops 1116307456 | bytes 10102784 | tf_op jit(solution)/shard_map/td,nd->tn/dot_general | solution.py:18
  190.7 156.4 %all-gather.3.cloned.1.call-done = bf16[4096,896]{1,0:T(8,128)(2,1)} async-done(((bf16[256,896]{1,0:T(8,128)(2,1)}), bf16[4096,896]{1,0:T(8,128)(2,1)}) %all-gather.3.cloned.1.call-update) | async-done | bytes 7340048 | tf_op jit(solution)/shard_map/all_gather | solution.py:49
  347.0 0.0 copy-start.1
  347.0 0.0 copy-start.2
  347.1 0.0 slice-start
  347.1 6.1 %convolution_multiply_fusion.2 = f32[4096,152]{0,1:T(8,128)S(1)} fusion(bf16[4096,896]{1,0:T(8,128)(2,1)} %all-gather.3.cloned.1.call-done, bf16[152,3,896]{2,0,1:T(8,128)(2,1)S(1)} %bitcast.26), kind=kOutput, calls=%fused_computation.2 | convolution fusion | flops 1116307456 | bytes 10102784 | tf_op jit(solution)/shard_map/td,nd->tn/dot_general | solution.py:27
  353.1 0.0 copy-done.1
  353.1 0.0 copy-done.2
  353.2 0.0 slice-start.1
  353.2 1.7 fusion.12
  354.8 0.0 slice-done
  354.8 0.4 slice-done.1
  355.3 1.7 fusion.14
  357.0 0.0 copy-start.4
  357.0 0.0 copy-start.5
  357.0 1.8 fusion.16
  358.8 0.0 copy-done.4
  358.8 0.0 copy-done.5
  358.9 1.4 convert_subtract_fusion
  360.2 3.1 collective-permute-start.1
  363.3 5.5 %collective-permute-start = (f32[1,152,3,896]{3,1,2,0:T(8,128)S(1)}, f32[1,152,3,896]{3,1,2,0:T(8,128)S(1)}, u32[]{:S(2)}, u32[]{:S(2)}) collective-permute-start(f32[1,152,3,896]{3,1,2,0:T(8,128)S(1)} %convert_subtract_fusion), channel_id=1, source_target_pairs={{496,0},{0,16},{16,32},{32,48},{48,64},{64,80},{80,96},{96,112},{1... | collective-permute-start | bytes 4902920 | tf_op jit(solution)/shard_map/ppermute | solution.py:12
  368.8 33.3 %collective-permute-done.1 = f32[1,152,3,896]{3,1,2,0:T(8,128)S(1)} collective-permute-done((f32[1,152,3,896]{3,1,2,0:T(8,128)S(1)}, f32[1,152,3,896]{3,1,2,0:T(8,128)S(1)}, u32[]{:S(2)}, u32[]{:S(2)}) %collective-permute-start.1) | collective-permute-done | bytes 1634336 | tf_op jit(solution)/shard_map/ppermute | solution.py:12
  402.1 2.3 collective-permute-done
  404.4 1.5 add_multiply_fusion
  (1 shorter events, 0.0 us)
Async XLA Ops:
  6.5 173.7 %all-gather.5.cloned.1.call-start = ((), (), s32[]{:S(2)}) async-start(), calls=%async_computation.1 | async-start | bytes 7798784 | tf_op jit(solution)/shard_map/all_gather | solution.py:48
  7.3 339.8 %all-gather.3.cloned.1.call-start = ((), (), s32[]{:S(2)}) async-start(), calls=%async_computation | async-start | bytes 7798784 | tf_op jit(solution)/shard_map/all_gather | solution.py:49
  180.2 6.1 %copy-start = (bf16[4096,896]{1,0:T(8,128)(2,1)S(1)}, bf16[4096,896]{1,0:T(8,128)(2,1)}, u32[]{:S(2)}) copy-start(bf16[4096,896]{1,0:T(8,128)(2,1)} %all-gather.5.cloned.1.call-done) | copy-start | bytes 22020100
  180.2 6.1 %copy-start.3 = (bf16[1,152,3,896]{3,1,2,0:T(8,128)(2,1)S(1)}, bf16[1,152,3,896]{3,1,2,0:T(8,128)(2,1)}, u32[]{:S(2)}) copy-start(bf16[1,152,3,896]{3,1,2,0:T(8,128)(2,1)} %param.7) | copy-start | bytes 2451460
  347.0 6.1 %copy-start.1 = (bf16[4096,896]{1,0:T(8,128)(2,1)S(1)}, bf16[4096,896]{1,0:T(8,128)(2,1)}, u32[]{:S(2)}) copy-start(bf16[4096,896]{1,0:T(8,128)(2,1)} %all-gather.3.cloned.1.call-done) | copy-start | bytes 22020100
  347.0 6.1 %copy-start.2 = (f32[4096,152]{0,1:T(8,128)S(1)}, f32[4096,152]{0,1:T(8,128)}, u32[]{:S(2)}) copy-start(f32[4096,152]{0,1:T(8,128)} %convolution_multiply_fusion) | copy-start | bytes 7471108
  347.1 7.8 %slice-start = ((s8[7340032]{0:T(1024)(128)(4,1)}), s8[4194304]{0:T(1024)(128)(4,1)S(1)}, s32[]{:S(2)}) async-start(s8[7340032]{0:T(1024)(128)(4,1)} %bitcast.22), calls=%async_computation.2 | async-start | bytes 8388608
  353.2 2.1 slice-start.1
  357.0 1.9 copy-start.4
  357.0 1.9 copy-start.5
  360.2 41.9 %collective-permute-start.1 = (f32[1,152,3,896]{3,1,2,0:T(8,128)S(1)}, f32[1,152,3,896]{3,1,2,0:T(8,128)S(1)}, u32[]{:S(2)}, u32[]{:S(2)}) collective-permute-start(f32[1,152,3,896]{3,1,2,0:T(8,128)S(1)} %convert_subtract_fusion), channel_id=1, source_target_pairs={{16,0},{32,16},{48,32},{64,48},{80,64},{96,80},{112,96},{128,112},... | collective-permute-start | bytes 4902920 | tf_op jit(solution)/shard_map/ppermute | solution.py:12
  363.3 41.1 %collective-permute-start = (f32[1,152,3,896]{3,1,2,0:T(8,128)S(1)}, f32[1,152,3,896]{3,1,2,0:T(8,128)S(1)}, u32[]{:S(2)}, u32[]{:S(2)}) collective-permute-start(f32[1,152,3,896]{3,1,2,0:T(8,128)S(1)} %convert_subtract_fusion), channel_id=1, source_target_pairs={{496,0},{0,16},{16,32},{32,48},{48,64},{64,80},{80,96},{96,112},{1... | collective-permute-start | bytes 4902920 | tf_op jit(solution)/shard_map/ppermute | solution.py:12
Sparse Core Ops, SparseCore 0:
  9.4 170.7 all-gather.4
  182.3 164.7 all-gather.2
where the time goes:
time: 416 us; the launch traced here: 413 us
  waiting for transfers between devices  366 us (88%)
  matrix products  21.7 us (5%)
  between operations  13.5 us (3%)
  starting transfers between devices  8.61 us (2%)
    all_gather x1, waiting for transfers between devices, on_device(): lax.all_gather(tokens, 'tp', axis=0, tiled=True)  172 us
    all_gather x1, waiting for transfers between devices, on_device(): lax.all_gather(cotangent, 'tp', axis=0, tiled=True)  156 us
    ppermute x2, waiting for transfers between devices, shifted(): return lax.ppermute(block, axis, route)  35.6 us
    ppermute x2, starting transfers between devices, shifted(): return lax.ppermute(block, axis, route)  8.57 us
  transfers between devices with their start and end apart: 4, of which 4 were waited for; matrix products, arithmetic and copies ran while one was open for 3% of the time, Pallas kernels for 0%

commit v1 on v0

v1 whole, which is shorter than its diff:
```python
import functools

import jax
import jax.numpy as jnp
from jax import lax
from jax.experimental import pallas as pl
from jax.experimental.pallas import tpu as pltpu
from jax.sharding import PartitionSpec as P

STEP = 10
MESH = pl.DeviceIdType.MESH
LINK = jnp.bfloat16
NEAR = (((1,), (1,)), ((), ()))


def kernel(
    n_blk,
    n_tp,
    hidden_scale,
    tok,
    cot,
    w,
    fm,
    sm,
    out,
    xs,
    gs,
    wb,
    wn,
    fmv,
    smv,
    acc,
    gsend,
    grecv,
    ssend,
    srecv,
    local_sem,
    x_send,
    x_recv,
    g_send,
    g_recv,
    w_send,
    w_recv,
    p_send,
    p_recv,
    s_send,
    s_recv,
):
    b, t = lax.axis_index("blk"), lax.axis_index("tp")
    units, width = w.shape[1], w.shape[2]
    width_scale = width ** (-0.5)
    scales = (width_scale, width_scale, hidden_scale)
    right = {"blk": b, "tp": lax.rem(t + 2, n_tp)}
    left = {"blk": b, "tp": lax.rem(t + n_tp - 2, n_tp)}
    partner = {"blk": b, "tp": t + 1 - 2 * lax.rem(t, 2)}
    following = {"blk": lax.rem(b + 1, n_blk), "tp": t}
    previous = {"blk": lax.rem(b + n_blk - 1, n_blk), "tp": t}

    def remote(src, dst, send, recv, device):
        return pltpu.make_async_remote_copy(
            src_ref=src,
            dst_ref=dst,
            send_sem=send,
            recv_sem=recv,
            device_id=device,
            device_id_type=MESH,
        )

    local = [
        pltpu.make_async_copy(src, dst, local_sem.at[i])
        for i, (src, dst) in enumerate(
            ((tok, xs.at[0]), (cot, gs.at[0]), (w, wb.at[0]), (fm, fmv), (sm, smv))
        )
    ]
    for copy in local:
        copy.start()

    barrier = pltpu.get_barrier_semaphore()
    for device in (right, left, partner, following, previous):
        pl.semaphore_signal(barrier, inc=1, device_id=device, device_id_type=MESH)
    pl.semaphore_wait(barrier, 5)

    def forward_x(src, dst, device):
        return remote(src, xs.at[dst], x_send.at[dst], x_recv.at[dst], device)

    def forward_g(src, dst, device):
        return remote(src, gs.at[dst], g_send.at[dst], g_recv.at[dst], device)

    moves = {}
    moves["x", 1] = forward_x(tok, 1, right)
    moves["g", 2] = forward_g(cot, 2, left)
    moves["g", 1] = forward_g(cot, 1, right)
    moves["x", 2] = forward_x(tok, 2, left)
    for move in moves.values():
        move.start()
    w_moves = [
        remote(w, wb.at[1], w_send.at[0], w_recv.at[0], partner),
        remote(w, wn.at[0], w_send.at[1], w_recv.at[1], following),
        remote(w, wn.at[1], w_send.at[2], w_recv.at[2], previous),
    ]
    for move in w_moves:
        move.start()

    acc[...] = jnp.zeros_like(acc)

    def compute(slot, half):
        x, g = xs[slot], gs[slot]

        def near(rows, data):
            return lax.dot_general(rows, data, NEAR, preferred_element_type=jnp.float32)

        gate = near(wb[half, 0], x) * width_scale
        upper = near(wb[half, 1], x) * width_scale
        back = near(wb[half, 2], g) * hidden_scale
        sigma = jax.nn.sigmoid(gate)
        swish = gate * sigma
        hidden = (swish * upper).astype(jnp.bfloat16)
        dgate = (back * upper * sigma * (1.0 + gate * (1.0 - sigma))).astype(jnp.bfloat16)
        dupper = (back * swish).astype(jnp.bfloat16)
        acc[half, 0] += jnp.dot(dgate, x, preferred_element_type=jnp.float32)
        acc[half, 1] += jnp.dot(dupper, x, preferred_element_type=jnp.float32)
        acc[half, 2] += jnp.dot(hidden, g, preferred_element_type=jnp.float32)

    def both_halves(first_slot, slots):
        @pl.loop(0, 2 * slots)
        def _(i):
            compute(first_slot + i // 2, 1 - i % 2)

    for copy in local:
        copy.wait()
    compute(0, 0)
    for step in (1, 2, 3):
        r, l = 2 * step - 1, 2 * step
        order = (("x", r), ("g", l), ("g", r), ("x", l))
        for kind, slot in order:
            moves[kind, slot].wait_recv()
            if step < 3:
                target, device = slot + 2, right if slot == r else left
            elif (kind, slot) == ("x", r):
                target, device = 7, right
            elif (kind, slot) == ("g", l):
                target, device = 7, left
            else:
                continue
            if kind == "x":
                moves[kind, target] = forward_x(xs.at[slot], target, device)
            else:
                moves[kind, target] = forward_g(gs.at[slot], target, device)
            moves[kind, target].start()
        if step == 1:
            w_moves[0].wait_recv()
            compute(0, 1)
        both_halves(r, 2)
    moves["x", 7].wait_recv()
    moves["g", 7].wait_recv()
    compute(7, 1)

    cut = units // 32 * 16 + 16
    pieces = [(m, pl.ds(lo, n)) for m in range(3) for lo, n in ((0, cut), (cut, units - cut))]
    p_moves = []
    for i, (m, rows) in enumerate(pieces):
        gsend[m, rows] = acc[1, m, rows].astype(LINK)
        p_moves.append(
            remote(gsend.at[m, rows], grecv.at[m, rows], p_send.at[i], p_recv.at[i], partner)
        )
        p_moves[-1].start()
    compute(7, 0)
    w_moves[1].wait_recv()
    w_moves[2].wait_recv()

    correct_one = 1.0 - 0.9**STEP
    correct_two = 1.0 - 0.95**STEP
    s_moves = []

    def adam(i):
        m, rows = pieces[i]
        p_moves[i].wait_recv()
        grad = (acc[0, m, rows] + grecv[m, rows].astype(jnp.float32)) * scales[m]
        one = 0.9 * fmv[m, rows].astype(jnp.float32) + 0.1 * grad
        two = 0.95 * smv[m, rows].astype(jnp.float32) + 0.05 * grad * grad
        step = one / correct_one / (jnp.sqrt(two / correct_two) + 1e-08)
        acc[0, m, rows] = step
        ssend[m, rows] = step.astype(LINK)
        for j, device in enumerate((following, previous)):
            move = remote(
                ssend.at[m, rows],
                srecv.at[j, m, rows],
                s_send.at[j, i],
                s_recv.at[j, i],
                device,
            )
            move.start()
            s_moves.append(move)

    def average(i):
        m, rows = pieces[i]
        s_moves[2 * i].wait_recv()
        s_moves[2 * i + 1].wait_recv()
        f32 = jnp.float32
        steps = acc[0, m, rows] + srecv[0, m, rows].astype(f32) + srecv[1, m, rows].astype(f32)
        rest = wb[0, m, rows].astype(f32) + wn[0, m, rows].astype(f32) + wn[1, m, rows].astype(f32)
        out[m, rows] = (0.99 * rest - 0.1 * steps) / 3.0

    lag = 2
    for i in range(len(pieces) + lag):
        if i < len(pieces):
            adam(i)
        if i >= lag:
            average(i - lag)
    for move in list(moves.values()) + w_moves + p_moves + s_moves:
        move.wait_send()


def on_device(n_blk, n_tp, tokens, cotangent, weights, first_moment, second_moment):
    rows, width = tokens.shape
    units = weights.shape[1]
    shape = (3, units, width)
    bf16, f32 = jnp.bfloat16, jnp.float32
    slots = n_tp // 2
    pieces = 6
    by_kind = [a[0].transpose(1, 0, 2) for a in (weights, first_moment, second_moment)]
    dma = pltpu.SemaphoreType.DMA
    averaged = pl.pallas_call(
        functools.partial(kernel, n_blk, n_tp, (units * n_tp) ** (-0.5)),
        out_shape=jax.ShapeDtypeStruct(shape, f32),
        in_specs=[pl.BlockSpec(memory_space=pl.ANY)] * 5,
        out_specs=pl.BlockSpec(memory_space=pltpu.VMEM),
        scratch_shapes=[
            pltpu.VMEM((slots, rows, width), bf16),
            pltpu.VMEM((slots, rows, width), bf16),
            pltpu.VMEM((2,) + shape, bf16),
            pltpu.VMEM((2,) + shape, bf16),
            pltpu.VMEM(shape, bf16),
            pltpu.VMEM(shape, bf16),
            pltpu.VMEM((2,) + shape, f32),
            pltpu.VMEM(shape, LINK),
            pltpu.VMEM(shape, LINK),
            pltpu.VMEM(shape, LINK),
            pltpu.VMEM((2,) + shape, LINK),
            dma((5,)),
            dma((slots,)),
            dma((slots,)),
            dma((slots,)),
            dma((slots,)),
            dma((3,)),
            dma((3,)),
            dma((pieces,)),
            dma((pieces,)),
            dma((2, pieces)),
            dma((2, pieces)),
        ],
        compiler_params=pltpu.CompilerParams(
            collective_id=0, has_side_effects=True, vmem_limit_bytes=60 << 20
        ),
    )(tokens, cotangent, *by_kind)
    return averaged.transpose(1, 0, 2)[None]


def solution(mesh):
    in_specs = (
        P(("blk", "tp"), None),
        P(("blk", "tp"), None),
        P("blk", "tp", None, None),
        P("blk", "tp", None, None),
        P("blk", "tp", None, None),
    )
    out_specs = P("blk", "tp", None, None)
    return jax.shard_map(
        functools.partial(on_device, mesh.shape["blk"], mesh.shape["tp"]),
        mesh=mesh,
        in_specs=in_specs,
        out_specs=out_specs,
        check_vma=False,
    )
```

time: 416 us -> 127 us (0.31)
  waiting for transfers between devices: 366 us -> 0 us
  Pallas kernels: 0 us -> 123 us
  matrix products: 21.7 us -> 0 us
  between operations: 13.5 us -> 0.01 us
  starting transfers between devices: 8.61 us -> 0 us
    all_gather x2 -> x0, waiting for transfers between devices: 329 us -> none  [the longest x1 172 us: on_device(): lax.all_gather(tokens, 'tp', axis=0, tiled=True)]
    pallas_call x0 -> x1, Pallas kernels: none -> 123 us  [on_device(): pl.pallas_call(functools.partial(kernel, n_blk, n_tp, (units * n_tp) ** (...]
    ppermute x2 -> x0, waiting for transfers between devices: 35.6 us -> none  [shifted(): return lax.ppermute(block, axis, route)]
    dot_general x6 -> x0, matrix products: 21.7 us -> none  [the longest x1 6.08 us: row_terms(): jnp.einsum('td,nd->tn', xs, rows[:, 1, :], preferred_element_type=jnp.flo...]
    ppermute x2 -> x0, starting transfers between devices: 8.57 us -> none  [shifted(): return lax.ppermute(block, axis, route)]
  transfers between devices with their start and end apart: 4 -> 0, of which waited for: 4 -> 0; matrix products, arithmetic and copies ran while one was open for 3% -> 0% of each run, Pallas kernels for 0% -> 0%
where the time goes in v1:
time: 127 us; the launch traced here: 126 us
  Pallas kernels  123 us (97%)
  local copies, waits for them, and re-layouts  2.7 us (2%)
    pallas_call x1, Pallas kernels, on_device(): pl.pallas_call(functools.partial(kernel, n_blk, n_tp, (units * n_tp) ** (...  123 us
    unnamed x1, local copies, waits for them, and re-layouts  2.7 us

profile of v1, /device:TPU:7, one launch (start us, length us, event | category | flops | bytes accessed | tf_op | source)
XLA Modules:
  0.0 125.7 jit_solution(10749177424333312022)
XLA Ops:
  0.0 123.0 %shard_map.55 = f32[3,152,896]{2,1,0:T(8,128)} custom-call(bf16[256,896]{1,0:T(8,128)(2,1)} %tok.1, bf16[256,896]{1,0:T(8,128)(2,1)} %cot.1, bf16[3,152,896]{2,1,0:T(8,128)(2,1)} %bitcast.13, bf16[3,152,896]{2,1,0:T(8,128)(2,1)} %bitcast.14, bf16[3,152,896]{2,1,0:T(8,128)(2,1)} %bitcast.15), custom_call_target="tpu_custom_call" | custom-call | tf_op jit(solution)/shard_map/pallas_call | solution.py:223
  123.0 2.7 %copy.7 = f32[1,152,3,896]{3,1,2,0:T(8,128)} copy(f32[1,152,3,896]{3,1,2,0:T(8,128)} %bitcast.12) | data formatting | bytes 3268608

commit v2 on v1

--- a/solution.py
+++ b/solution.py
@@ -8,9 +8,16 @@
 from jax.sharding import PartitionSpec as P
 
 STEP = 10
+ROW = 8
+PARTS = 3
 MESH = pl.DeviceIdType.MESH
 LINK = jnp.bfloat16
 NEAR = (((1,), (1,)), ((), ()))
+
+
+def cuts(units):
+    size = units // PARTS // 16 * 16
+    return [(i * size, size if i < PARTS - 1 else units - i * size) for i in range(PARTS)]
 
 
 def kernel(
@@ -34,6 +41,7 @@
     grecv,
     ssend,
     srecv,
+    relayed,
     local_sem,
     x_send,
     x_recv,
@@ -45,6 +53,8 @@
     p_recv,
     s_send,
     s_recv,
+    r_send,
+    r_recv,
 ):
     b, t = lax.axis_index("blk"), lax.axis_index("tp")
     units, width = w.shape[1], w.shape[2]
@@ -56,6 +66,14 @@
     following = {"blk": lax.rem(b + 1, n_blk), "tp": t}
     previous = {"blk": lax.rem(b + n_blk - 1, n_blk), "tp": t}
 
+    place = lax.rem(b, ROW)
+    even = lax.rem(t, 2) == 0
+    last = jnp.logical_and(place == ROW - 1, even)
+    first = jnp.logical_and(place == 0, even)
+    up = {"blk": lax.rem(b + ROW, n_blk), "tp": t}
+    down = {"blk": lax.rem(b + n_blk - ROW, n_blk), "tp": t}
+    across = {"blk": lax.rem(b + n_blk + ROW - 1 - 2 * place, n_blk), "tp": t}
+
     def remote(src, dst, send, recv, device):
         return pltpu.make_async_remote_copy(
             src_ref=src,
@@ -78,7 +96,17 @@
     barrier = pltpu.get_barrier_semaphore()
     for device in (right, left, partner, following, previous):
         pl.semaphore_signal(barrier, inc=1, device_id=device, device_id_type=MESH)
-    pl.semaphore_wait(barrier, 5)
+    wraps_round = jnp.logical_or(last, first)
+
+    @pl.when(jnp.logical_not(wraps_round))
+    def _():
+        pl.semaphore_wait(barrier, 5)
+
+    @pl.when(wraps_round)
+    def _():
+        for device in (up, down, across):
+            pl.semaphore_signal(barrier, inc=1, device_id=device, device_id_type=MESH)
+        pl.semaphore_wait(barrier, 8)
 
     def forward_x(src, dst, device):
         return remote(src, xs.at[dst], x_send.at[dst], x_recv.at[dst], device)
@@ -155,8 +183,7 @@
     moves["g", 7].wait_recv()
     compute(7, 1)
 
-    cut = units // 32 * 16 + 16
-    pieces = [(m, pl.ds(lo, n)) for m in range(3) for lo, n in ((0, cut), (cut, units - cut))]
+    pieces = [(m, pl.ds(lo, n)) for m in range(3) for lo, n in cuts(units)]
     p_moves = []
     for i, (m, rows) in enumerate(pieces):
         gsend[m, rows] = acc[1, m, rows].astype(LINK)
@@ -181,7 +208,8 @@
         step = one / correct_one / (jnp.sqrt(two / correct_two) + 1e-08)
         acc[0, m, rows] = step
         ssend[m, rows] = step.astype(LINK)
-        for j, device in enumerate((following, previous)):
+        ends = ((following, last, up), (previous, first, down))
+        for j, (device, wraps, relay) in enumerate(ends):
             move = remote(
                 ssend.at[m, rows],
                 srecv.at[j, m, rows],
@@ -189,8 +217,33 @@
                 s_recv.at[j, i],
                 device,
             )
-            move.start()
             s_moves.append(move)
+            pl.when(jnp.logical_not(wraps))(move.start)
+            detour = remote(
+                ssend.at[m, rows],
+                relayed.at[m, rows],
+                s_send.at[j, i],
+                r_recv.at[i],
+                relay,
+            )
+            pl.when(wraps)(detour.start)
+
+    def relay_on(i, j):
+        m, rows = pieces[i]
+        return remote(
+            relayed.at[m, rows], srecv.at[j, m, rows], r_send.at[i], s_recv.at[j, i], across
+        )
+
+    def relay(i):
+        m, rows = pieces[i]
+        for j, (wraps, device) in enumerate(((last, up), (first, down))):
+
+            @pl.when(wraps)
+            def _(j=j, device=device):
+                remote(
+                    relayed.at[m, rows], relayed.at[m, rows], r_send.at[i], r_recv.at[i], device
+                ).wait_recv()
+                relay_on(i, j).start()
 
     def average(i):
         m, rows = pieces[i]
@@ -199,16 +252,22 @@
         f32 = jnp.float32
         steps = acc[0, m, rows] + srecv[0, m, rows].astype(f32) + srecv[1, m, rows].astype(f32)
         rest = wb[0, m, rows].astype(f32) + wn[0, m, rows].astype(f32) + wn[1, m, rows].astype(f32)
-        out[m, rows] = (0.99 * rest - 0.1 * steps) / 3.0
-
-    lag = 2
-    for i in range(len(pieces) + lag):
+        out[m, rows] = 0.99 * rest - 0.1 * steps
+
+    for i in range(len(pieces) + 4):
         if i < len(pieces):
             adam(i)
-        if i >= lag:
-            average(i - lag)
+        if 0 <= i - 2 < len(pieces):
+            relay(i - 2)
+        if i >= 4:
+            average(i - 4)
     for move in list(moves.values()) + w_moves + p_moves + s_moves:
         move.wait_send()
+
+    @pl.when(wraps_round)
+    def _():
+        for i in range(len(pieces)):
+            relay_on(i, 0).wait_send()
 
 
 def on_device(n_blk, n_tp, tokens, cotangent, weights, first_moment, second_moment):
@@ -217,13 +276,14 @@
     shape = (3, units, width)
     bf16, f32 = jnp.bfloat16, jnp.float32
     slots = n_tp // 2
-    pieces = 6
+    pieces = 3 * PARTS
     by_kind = [a[0].transpose(1, 0, 2) for a in (weights, first_moment, second_moment)]
     dma = pltpu.SemaphoreType.DMA
-    averaged = pl.pallas_call(
+    arrays = [pltpu.with_memory_space_constraint(a, pltpu.HBM) for a in (tokens, cotangent, *by_kind)]
+    total = pl.pallas_call(
         functools.partial(kernel, n_blk, n_tp, (units * n_tp) ** (-0.5)),
         out_shape=jax.ShapeDtypeStruct(shape, f32),
-        in_specs=[pl.BlockSpec(memory_space=pl.ANY)] * 5,
+        in_specs=[pl.BlockSpec(memory_space=pltpu.HBM)] * 5,
         out_specs=pl.BlockSpec(memory_space=pltpu.VMEM),
         scratch_shapes=[
             pltpu.VMEM((slots, rows, width), bf16),
@@ -237,6 +297,7 @@
             pltpu.VMEM(shape, LINK),
             pltpu.VMEM(shape, LINK),
             pltpu.VMEM((2,) + shape, LINK),
+            pltpu.VMEM(shape, LINK),
             dma((5,)),
             dma((slots,)),
             dma((slots,)),
@@ -248,12 +309,14 @@
             dma((pieces,)),
             dma((2, pieces)),
             dma((2, pieces)),
+            dma((pieces,)),
+            dma((pieces,)),
         ],
         compiler_params=pltpu.CompilerParams(
-            collective_id=0, has_side_effects=True, vmem_limit_bytes=60 << 20
+            collective_id=0, has_side_effects=True, vmem_limit_bytes=36 << 20
         ),
-    )(tokens, cotangent, *by_kind)
-    return averaged.transpose(1, 0, 2)[None]
+    )(*arrays)
+    return (total / 3.0).transpose(1, 0, 2)[None]
 
 
 def solution(mesh):

time: 127 us -> 129 us (1.016)
  Pallas kernels: 123 us -> 127 us
  local copies, waits for them, and re-layouts: 2.7 us -> 0 us
  other arithmetic: 0 us -> 1.3 us
    pallas_call x1, Pallas kernels: 123 us -> 127 us  [on_device(): pl.pallas_call(functools.partial(kernel, n_blk, n_tp, (units * n_tp) ** (...]
    unnamed x1 -> x0, local copies, waits for them, and re-layouts: 2.7 us -> none
    broadcast_in_dim x0 -> x1, other arithmetic: none -> 1.3 us  [on_device(): return (total / 3.0).transpose(1, 0, 2)[None]]
where the time goes in v2:
time: 129 us
  Pallas kernels  127 us (98%)
  other arithmetic  1.3 us (1%)
    pallas_call x1, Pallas kernels, on_device(): pl.pallas_call(functools.partial(kernel, n_blk, n_tp, (units * n_tp) ** (...  127 us

profile of v2, /device:TPU:7, one launch (start us, length us, event | category | flops | bytes accessed | tf_op | source)
XLA Modules:
  0.0 128.6 jit_solution(15565284852547494367)
XLA Ops:
  0.0 127.3 %shard_map.55 = f32[3,152,896]{2,1,0:T(8,128)S(1)} custom-call(bf16[256,896]{1,0:T(8,128)(2,1)} %tok.1, bf16[256,896]{1,0:T(8,128)(2,1)} %cot.1, bf16[3,152,896]{2,1,0:T(8,128)(2,1)} %bitcast.13, bf16[3,152,896]{2,1,0:T(8,128)(2,1)} %bitcast.14, bf16[3,152,896]{2,1,0:T(8,128)(2,1)} %bitcast.15), custom_call_target="tpu_custom_call" | custom-call | tf_op jit(solution)/shard_map/pallas_call | solution.py:283
  127.3 1.3 %multiply_bitcast_fusion = f32[1,152,3,896]{3,1,2,0:T(8,128)} fusion(f32[3,152,896]{2,1,0:T(8,128)S(1)} %shard_map.55), kind=kLoop, calls=%fused_computation | loop fusion | flops 408576 | bytes 3268608 | tf_op jit(solution)/shard_map/broadcast_in_dim | solution.py:319

commit v3 on v2

--- a/solution.py
+++ b/solution.py
@@ -10,6 +10,7 @@
 STEP = 10
 ROW = 8
 PARTS = 3
+LATE = 32
 MESH = pl.DeviceIdType.MESH
 LINK = jnp.bfloat16
 NEAR = (((1,), (1,)), ((), ()))
@@ -32,6 +33,8 @@
     out,
     xs,
     gs,
+    lx,
+    lg,
     wb,
     wn,
     fmv,
@@ -47,6 +50,10 @@
     x_recv,
     g_send,
     g_recv,
+    lx_send,
+    lx_recv,
+    lg_send,
+    lg_recv,
     w_send,
     w_recv,
     p_send,
@@ -59,6 +66,7 @@
     b, t = lax.axis_index("blk"), lax.axis_index("tp")
     units, width = w.shape[1], w.shape[2]
     width_scale = width ** (-0.5)
+    soon, late = pl.ds(0, tok.shape[0] - LATE), pl.ds(tok.shape[0] - LATE, LATE)
     scales = (width_scale, width_scale, hidden_scale)
     right = {"blk": b, "tp": lax.rem(t + 2, n_tp)}
     left = {"blk": b, "tp": lax.rem(t + n_tp - 2, n_tp)}
@@ -87,7 +95,15 @@
     local = [
         pltpu.make_async_copy(src, dst, local_sem.at[i])
         for i, (src, dst) in enumerate(
-            ((tok, xs.at[0]), (cot, gs.at[0]), (w, wb.at[0]), (fm, fmv), (sm, smv))
+            (
+                (tok.at[soon], xs.at[0]),
+                (cot.at[soon], gs.at[0]),
+                (w, wb.at[0]),
+                (fm, fmv),
+                (sm, smv),
+                (tok.at[late], lx.at[pl.ds(0, LATE)]),
+                (cot.at[late], lg.at[pl.ds(0, LATE)]),
+            )
         )
     ]
     for copy in local:
@@ -114,12 +130,24 @@
     def forward_g(src, dst, device):
         return remote(src, gs.at[dst], g_send.at[dst], g_recv.at[dst], device)
 
+    def of_slot(slot):
+        return pl.ds(2 * LATE * slot, 2 * LATE)
+
+    def forward_late(kind, src, dst, device):
+        held, send, recv = (lx, lx_send, lx_recv) if kind == "x" else (lg, lg_send, lg_recv)
+        return remote(held.at[of_slot(src)], held.at[of_slot(dst)], send.at[dst], recv.at[dst], device)
+
     moves = {}
-    moves["x", 1] = forward_x(tok, 1, right)
-    moves["g", 2] = forward_g(cot, 2, left)
-    moves["g", 1] = forward_g(cot, 1, right)
-    moves["x", 2] = forward_x(tok, 2, left)
-    for move in moves.values():
+    moves["x", 1] = forward_x(tok.at[soon], 1, right)
+    moves["g", 2] = forward_g(cot.at[soon], 2, left)
+    moves["g", 1] = forward_g(cot.at[soon], 1, right)
+    moves["x", 2] = forward_x(tok.at[soon], 2, left)
+    other = pl.ds(LATE, LATE)
+    lates = {
+        ("x", 0): remote(tok.at[late], lx.at[other], lx_send.at[0], lx_recv.at[0], partner),
+        ("g", 0): remote(cot.at[late], lg.at[other], lg_send.at[0], lg_recv.at[0], partner),
+    }
+    for move in list(moves.values()) + list(lates.values()):
         move.start()
     w_moves = [
         remote(w, wb.at[1], w_send.at[0], w_recv.at[0], partner),
@@ -132,7 +160,9 @@
     acc[...] = jnp.zeros_like(acc)
 
     def compute(slot, half):
-        x, g = xs[slot], gs[slot]
+        add_terms(xs[slot], gs[slot], half)
+
+    def add_terms(x, g, half):
 
         def near(rows, data):
             return lax.dot_general(rows, data, NEAR, preferred_element_type=jnp.float32)
@@ -175,6 +205,12 @@
             else:
                 moves[kind, target] = forward_g(gs.at[slot], target, device)
             moves[kind, target].start()
+        if step == 3:
+            for kind in ("x", "g"):
+                lates[kind, 0].wait_recv()
+            for kind, dst, device in (("x", 1, right), ("g", 2, left), ("g", 1, right), ("x", 2, left)):
+                lates[kind, dst] = forward_late(kind, 0, dst, device)
+                lates[kind, dst].start()
         if step == 1:
             w_moves[0].wait_recv()
             compute(0, 1)
@@ -192,6 +228,26 @@
         )
         p_moves[-1].start()
     compute(7, 0)
+
+    def add_late(pair):
+        rows = pl.ds(4 * LATE * pair, 4 * LATE)
+        add_terms(lx[rows], lg[rows], 0)
+
+    for step in (1, 2, 3):
+        r, l = 2 * step - 1, 2 * step
+        for kind, slot in (("x", r), ("g", l), ("g", r), ("x", l)):
+            lates[kind, slot].wait_recv()
+            target, device = slot + 2, right if slot == r else left
+            if step == 3:
+                if (kind, slot) not in (("x", r), ("g", l)):
+                    continue
+                target = 7
+            lates[kind, target] = forward_late(kind, slot, target, device)
+            lates[kind, target].start()
+        add_late(step - 1)
+    for kind in ("x", "g"):
+        lates[kind, 7].wait_recv()
+    add_late(3)
     w_moves[1].wait_recv()
     w_moves[2].wait_recv()
 
@@ -208,7 +264,7 @@
         step = one / correct_one / (jnp.sqrt(two / correct_two) + 1e-08)
         acc[0, m, rows] = step
         ssend[m, rows] = step.astype(LINK)
-        ends = ((following, last, up), (previous, first, down))
+        ends = ((following, last, across), (previous, first, across))
         for j, (device, wraps, relay) in enumerate(ends):
             move = remote(
                 ssend.at[m, rows],
@@ -228,22 +284,22 @@
             )
             pl.when(wraps)(detour.start)
 
-    def relay_on(i, j):
+    def relay_on(i, j, device):
         m, rows = pieces[i]
         return remote(
-            relayed.at[m, rows], srecv.at[j, m, rows], r_send.at[i], s_recv.at[j, i], across
+            relayed.at[m, rows], srecv.at[j, m, rows], r_send.at[i], s_recv.at[j, i], device
         )
 
     def relay(i):
         m, rows = pieces[i]
-        for j, (wraps, device) in enumerate(((last, up), (first, down))):
+        for j, (wraps, device) in enumerate(((first, up), (last, down))):
 
             @pl.when(wraps)
             def _(j=j, device=device):
                 remote(
-                    relayed.at[m, rows], relayed.at[m, rows], r_send.at[i], r_recv.at[i], device
+                    relayed.at[m, rows], relayed.at[m, rows], r_send.at[i], r_recv.at[i], across
                 ).wait_recv()
-                relay_on(i, j).start()
+                relay_on(i, j, device).start()
 
     def average(i):
         m, rows = pieces[i]
@@ -261,13 +317,13 @@
             relay(i - 2)
         if i >= 4:
             average(i - 4)
-    for move in list(moves.values()) + w_moves + p_moves + s_moves:
+    for move in list(moves.values()) + list(lates.values()) + w_moves + p_moves + s_moves:
         move.wait_send()
 
     @pl.when(wraps_round)
     def _():
         for i in range(len(pieces)):
-            relay_on(i, 0).wait_send()
+            relay_on(i, 0, across).wait_send()
 
 
 def on_device(n_blk, n_tp, tokens, cotangent, weights, first_moment, second_moment):
@@ -286,8 +342,10 @@
         in_specs=[pl.BlockSpec(memory_space=pltpu.HBM)] * 5,
         out_specs=pl.BlockSpec(memory_space=pltpu.VMEM),
         scratch_shapes=[
-            pltpu.VMEM((slots, rows, width), bf16),
-            pltpu.VMEM((slots, rows, width), bf16),
+            pltpu.VMEM((slots, rows - LATE, width), bf16),
+            pltpu.VMEM((slots, rows - LATE, width), bf16),
+            pltpu.VMEM((slots * 2 * LATE, width), bf16),
+            pltpu.VMEM((slots * 2 * LATE, width), bf16),
             pltpu.VMEM((2,) + shape, bf16),
             pltpu.VMEM((2,) + shape, bf16),
             pltpu.VMEM(shape, bf16),
@@ -298,7 +356,11 @@
             pltpu.VMEM(shape, LINK),
             pltpu.VMEM((2,) + shape, LINK),
             pltpu.VMEM(shape, LINK),
-            dma((5,)),
+            dma((7,)),
+            dma((slots,)),
+            dma((slots,)),
+            dma((slots,)),
+            dma((slots,)),
             dma((slots,)),
             dma((slots,)),
             dma((slots,)),

time: 129 us -> 116 us (0.90)
  Pallas kernels: 127 us -> 115 us
    pallas_call x1, Pallas kernels: 127 us -> 115 us  [on_device(): pl.pallas_call(functools.partial(kernel, n_blk, n_tp, (units * n_tp) ** (...]
where the time goes in v3:
time: 116 us
  Pallas kernels  115 us (99%)
  other arithmetic  1.3 us (1%)
    pallas_call x1, Pallas kernels, on_device(): pl.pallas_call(functools.partial(kernel, n_blk, n_tp, (units * n_tp) ** (...  115 us

profile of v3, /device:TPU:7, one launch (start us, length us, event | category | flops | bytes accessed | tf_op | source)
XLA Modules:
  0.0 115.8 jit_solution(3378118837709719352)
XLA Ops:
  0.0 114.5 %shard_map.55 = f32[3,152,896]{2,1,0:T(8,128)S(1)} custom-call(bf16[256,896]{1,0:T(8,128)(2,1)} %tok.1, bf16[256,896]{1,0:T(8,128)(2,1)} %cot.1, bf16[3,152,896]{2,1,0:T(8,128)(2,1)} %bitcast.13, bf16[3,152,896]{2,1,0:T(8,128)(2,1)} %bitcast.14, bf16[3,152,896]{2,1,0:T(8,128)(2,1)} %bitcast.15), custom_call_target="tpu_custom_call" | custom-call | tf_op jit(solution)/shard_map/pallas_call | solution.py:339
  114.5 1.3 %multiply_bitcast_fusion = f32[1,152,3,896]{3,1,2,0:T(8,128)} fusion(f32[3,152,896]{2,1,0:T(8,128)S(1)} %shard_map.55), kind=kLoop, calls=%fused_computation | loop fusion | flops 408576 | bytes 3268608 | tf_op jit(solution)/shard_map/broadcast_in_dim | solution.py:381

commit v4 on v3

--- a/solution.py
+++ b/solution.py
@@ -75,9 +75,7 @@
     previous = {"blk": lax.rem(b + n_blk - 1, n_blk), "tp": t}
 
     place = lax.rem(b, ROW)
-    even = lax.rem(t, 2) == 0
-    last = jnp.logical_and(place == ROW - 1, even)
-    first = jnp.logical_and(place == 0, even)
+    last, first = place == ROW - 1, place == 0
     up = {"blk": lax.rem(b + ROW, n_blk), "tp": t}
     down = {"blk": lax.rem(b + n_blk - ROW, n_blk), "tp": t}
     across = {"blk": lax.rem(b + n_blk + ROW - 1 - 2 * place, n_blk), "tp": t}
@@ -254,6 +252,7 @@
     correct_one = 1.0 - 0.9**STEP
     correct_two = 1.0 - 0.95**STEP
     s_moves = []
+    detours = range(1, len(pieces), 2)
 
     def adam(i):
         m, rows = pieces[i]
@@ -274,6 +273,9 @@
                 device,
             )
             s_moves.append(move)
+            if i not in detours:
+                move.start()
+                continue
             pl.when(jnp.logical_not(wraps))(move.start)
             detour = remote(
                 ssend.at[m, rows],
@@ -310,19 +312,18 @@
         rest = wb[0, m, rows].astype(f32) + wn[0, m, rows].astype(f32) + wn[1, m, rows].astype(f32)
         out[m, rows] = 0.99 * rest - 0.1 * steps
 
-    for i in range(len(pieces) + 4):
-        if i < len(pieces):
-            adam(i)
-        if 0 <= i - 2 < len(pieces):
-            relay(i - 2)
-        if i >= 4:
-            average(i - 4)
+    for i in range(len(pieces)):
+        adam(i)
+    for i in detours:
+        relay(i)
+    for i in range(len(pieces)):
+        average(i)
     for move in list(moves.values()) + list(lates.values()) + w_moves + p_moves + s_moves:
         move.wait_send()
 
     @pl.when(wraps_round)
     def _():
-        for i in range(len(pieces)):
+        for i in detours:
             relay_on(i, 0, across).wait_send()
 
 

time: 116 us -> 112 us (0.966)
  the two profiles are of different devices: /device:TPU:7 before, /device:TPU:64 now
where the time goes in v4:
time: 112 us
  Pallas kernels  111 us (99%)
  other arithmetic  1.3 us (1%)
    pallas_call x1, Pallas kernels, on_device(): pl.pallas_call(functools.partial(kernel, n_blk, n_tp, (units * n_tp) ** (...  111 us

profile of v4, /device:TPU:64, one launch (start us, length us, event | category | flops | bytes accessed | tf_op | source)
XLA Modules:
  0.0 112.1 jit_solution(3082047336758717155)
XLA Ops:
  0.0 110.8 %shard_map.55 = f32[3,152,896]{2,1,0:T(8,128)S(1)} custom-call(bf16[256,896]{1,0:T(8,128)(2,1)} %tok.1, bf16[256,896]{1,0:T(8,128)(2,1)} %cot.1, bf16[3,152,896]{2,1,0:T(8,128)(2,1)} %bitcast.13, bf16[3,152,896]{2,1,0:T(8,128)(2,1)} %bitcast.14, bf16[3,152,896]{2,1,0:T(8,128)(2,1)} %bitcast.15), custom_call_target="tpu_custom_call" | custom-call | tf_op jit(solution)/shard_map/pallas_call | solution.py:340
  110.8 1.3 %multiply_bitcast_fusion = f32[1,152,3,896]{3,1,2,0:T(8,128)} fusion(f32[3,152,896]{2,1,0:T(8,128)S(1)} %shard_map.55), kind=kLoop, calls=%fused_computation | loop fusion | flops 408576 | bytes 3268608 | tf_op jit(solution)/shard_map/broadcast_in_dim | solution.py:382

commit v5 on v4

--- a/solution.py
+++ b/solution.py
@@ -104,12 +104,11 @@
             )
         )
     ]
+    barrier = pltpu.get_barrier_semaphore()
+    for device in (following, previous, right, left, partner):
+        pl.semaphore_signal(barrier, inc=1, device_id=device, device_id_type=MESH)
     for copy in local:
         copy.start()
-
-    barrier = pltpu.get_barrier_semaphore()
-    for device in (right, left, partner, following, previous):
-        pl.semaphore_signal(barrier, inc=1, device_id=device, device_id_type=MESH)
     wraps_round = jnp.logical_or(last, first)
 
     @pl.when(jnp.logical_not(wraps_round))
@@ -157,10 +156,10 @@
 
     acc[...] = jnp.zeros_like(acc)
 
-    def compute(slot, half):
-        add_terms(xs[slot], gs[slot], half)
-
-    def add_terms(x, g, half):
+    def compute(slot, half, then=None):
+        add_terms(xs[slot], gs[slot], half, then)
+
+    def add_terms(x, g, half, then=None):
 
         def near(rows, data):
             return lax.dot_general(rows, data, NEAR, preferred_element_type=jnp.float32)
@@ -173,9 +172,10 @@
         hidden = (swish * upper).astype(jnp.bfloat16)
         dgate = (back * upper * sigma * (1.0 + gate * (1.0 - sigma))).astype(jnp.bfloat16)
         dupper = (back * swish).astype(jnp.bfloat16)
-        acc[half, 0] += jnp.dot(dgate, x, preferred_element_type=jnp.float32)
-        acc[half, 1] += jnp.dot(dupper, x, preferred_element_type=jnp.float32)
-        acc[half, 2] += jnp.dot(hidden, g, preferred_element_type=jnp.float32)
+        for m, (rows, data) in enumerate(((dgate, x), (dupper, x), (hidden, g))):
+            acc[half, m] += jnp.dot(rows, data, preferred_element_type=jnp.float32)
+            if then is not None:
+                then(m)
 
     def both_halves(first_slot, slots):
         @pl.loop(0, 2 * slots)
@@ -215,21 +215,26 @@
         both_halves(r, 2)
     moves["x", 7].wait_recv()
     moves["g", 7].wait_recv()
-    compute(7, 1)
 
     pieces = [(m, pl.ds(lo, n)) for m in range(3) for lo, n in cuts(units)]
     p_moves = []
-    for i, (m, rows) in enumerate(pieces):
-        gsend[m, rows] = acc[1, m, rows].astype(LINK)
-        p_moves.append(
-            remote(gsend.at[m, rows], grecv.at[m, rows], p_send.at[i], p_recv.at[i], partner)
-        )
-        p_moves[-1].start()
+
+    def give(of):
+        for i, (m, rows) in enumerate(pieces):
+            if m != of:
+                continue
+            gsend[m, rows] = acc[1, m, rows].astype(LINK)
+            p_moves.append(
+                remote(gsend.at[m, rows], grecv.at[m, rows], p_send.at[i], p_recv.at[i], partner)
+            )
+            p_moves[-1].start()
+
+    compute(7, 1, give)
     compute(7, 0)
 
-    def add_late(pair):
+    def add_late(pair, then=None):
         rows = pl.ds(4 * LATE * pair, 4 * LATE)
-        add_terms(lx[rows], lg[rows], 0)
+        add_terms(lx[rows], lg[rows], 0, then)
 
     for step in (1, 2, 3):
         r, l = 2 * step - 1, 2 * step
@@ -245,14 +250,11 @@
         add_late(step - 1)
     for kind in ("x", "g"):
         lates[kind, 7].wait_recv()
-    add_late(3)
-    w_moves[1].wait_recv()
-    w_moves[2].wait_recv()
 
     correct_one = 1.0 - 0.9**STEP
     correct_two = 1.0 - 0.95**STEP
     s_moves = []
-    detours = range(1, len(pieces), 2)
+    detours = (0, 2, 4, 6)
 
     def adam(i):
         m, rows = pieces[i]
@@ -312,8 +314,14 @@
         rest = wb[0, m, rows].astype(f32) + wn[0, m, rows].astype(f32) + wn[1, m, rows].astype(f32)
         out[m, rows] = 0.99 * rest - 0.1 * steps
 
-    for i in range(len(pieces)):
-        adam(i)
+    def finish(of):
+        for i, (m, _) in enumerate(pieces):
+            if m == of:
+                adam(i)
+
+    add_late(3, finish)
+    w_moves[1].wait_recv()
+    w_moves[2].wait_recv()
     for i in detours:
         relay(i)
     for i in range(len(pieces)):

time: 112 us -> 112 us (level)
  no operation moved by 1% of the time
where the time goes in v5:
time: 112 us
  Pallas kernels  111 us (99%)
  other arithmetic  1.3 us (1%)
    pallas_call x1, Pallas kernels, on_device(): pl.pallas_call(functools.partial(kernel, n_blk, n_tp, (units * n_tp) ** (...  111 us

profile of v5, /device:TPU:64, one launch (start us, length us, event | category | flops | bytes accessed | tf_op | source)
XLA Modules:
  0.0 112.3 jit_solution(12617708297693549226)
XLA Ops:
  0.0 110.9 %shard_map.55 = f32[3,152,896]{2,1,0:T(8,128)S(1)} custom-call(bf16[256,896]{1,0:T(8,128)(2,1)} %tok.1, bf16[256,896]{1,0:T(8,128)(2,1)} %cot.1, bf16[3,152,896]{2,1,0:T(8,128)(2,1)} %bitcast.13, bf16[3,152,896]{2,1,0:T(8,128)(2,1)} %bitcast.14, bf16[3,152,896]{2,1,0:T(8,128)(2,1)} %bitcast.15), custom_call_target="tpu_custom_call" | custom-call | tf_op jit(solution)/shard_map/pallas_call | solution.py:348
  110.9 1.3 %multiply_bitcast_fusion = f32[1,152,3,896]{3,1,2,0:T(8,128)} fusion(f32[3,152,896]{2,1,0:T(8,128)S(1)} %shard_map.55), kind=kLoop, calls=%fused_computation | loop fusion | flops 408576 | bytes 3268608 | tf_op jit(solution)/shard_map/broadcast_in_dim | solution.py:390
